TPU v7x, 32 devices: a whole 2x2x4 slice. The times are simulated.
32 devices in a mesh: dp: 16 (over z, y, core), mp: 2 (over x).
Axes of the slice: x: 2, y: 2, z: 4, core: 2. Of those that a mesh axis runs over, the one named last changes fastest.
Arguments:
- tokens: bfloat16 [2048, 2048], P(('dp', 'mp')), may hold values from -6 to 6
- lengths: int32 [22], replicated, may hold values from 1 to 1024, 2048 in all
- w_in: bfloat16 [2048, 2048], P('dp'), may hold values from -0.125 to 0.125
- w_forget: bfloat16 [2048, 2048], P('dp'), may hold values from -0.125 to 0.125
- w_gate: bfloat16 [2048, 2048], P('dp'), may hold values from -0.125 to 0.125
- w_out: bfloat16 [2048, 2048], P('dp'), may hold values from -0.125 to 0.125
- attn_gain: bfloat16 [2048], P('dp'), may hold values from 0.5 to 1.5
- mix_gain: bfloat16 [2048], P('dp'), may hold values from 0.5 to 1.5
- bound_table: bfloat16 [24, 2048], P(None, 'dp'), may hold values from -14 to 3
- ff_gate: bfloat16 [2048, 5632], P('dp', 'mp'), may hold values from -0.125 to 0.125
- ff_up: bfloat16 [2048, 5632], P('dp', 'mp'), may hold values from -0.125 to 0.125
- ff_down: bfloat16 [5632, 2048], P('mp', 'dp'), may hold values from -0.078125 to 0.078125
- mlp_gain: bfloat16 [2048], P('dp'), may hold values from 0.5 to 1.5
- out_grad: bfloat16 [2048, 2048], P(('dp', 'mp')), may hold values from -6 to 6
Outputs:
- result: bfloat16 [2048, 2048], P(('dp', 'mp'))
- token_grad: float32 [2048, 2048], P(('dp', 'mp'))
- grad_w_in: float32 [2048, 2048], P('dp')
- grad_w_forget: float32 [2048, 2048], P('dp')
- grad_w_gate: float32 [2048, 2048], P('dp')
- grad_w_out: float32 [2048, 2048], P('dp')
- grad_attn_gain: float32 [2048], P('dp')
- grad_mix_gain: float32 [2048], P('dp')
- grad_bound_table: float32 [24, 2048], P(None, 'dp')
- grad_ff_gate: float32 [2048, 5632], P('dp', 'mp')
- grad_ff_up: float32 [2048, 5632], P('dp', 'mp')
- grad_ff_down: float32 [5632, 2048], P('mp', 'dp')
- grad_mlp_gain: float32 [2048], P('dp')
Inputs may be any that keep to these rules, and one draw needn't show every extreme that they name: lengths of 22 sequences packed end to end; they sum to 2048 and the longest is 1024.
All inputs are finite; a program needn't handle non-finite values.
Results may differ from a plain program's by a relative error of at most 0.0085.
Values may be sent and summed in bfloat16 or wider, within the bound.
No kernel may reach another device: no remote copies, remote signals or barrier semaphores. Data moves between devices by JAX's collectives and lax.ppermute only.
A program may use at most 384 MiB of HBM per device.

v0:
```python
import jax
import jax.numpy as jnp
from jax import lax
from jax.sharding import PartitionSpec as P

LAYER = 12
epsilon = 1e-06


def entering(value, axis, join, neutral, backward):
    count, mine = (lax.axis_size(axis), lax.axis_index(axis))
    pieces = jax.tree.map(lambda part: lax.all_gather(part, axis), value)
    if backward:
        pieces = jax.tree.map(lambda part: part[::-1], pieces)
        mine = count - 1 - mine
    running = jax.tree.map(
        lambda part, zero: jnp.full_like(part, 0) + jnp.asarray(zero, part.dtype), value, neutral
    )

    def turn(position, running):
        longer = join(running, jax.tree.map(lambda part: part[position], pieces))
        return jax.tree.map(lambda new, old: jnp.where(position < mine, new, old), longer, running)

    return lax.fori_loop(0, count - 1, turn, running)


def contract_rows(left, right):
    return lax.dot_general(
        left, right, (((0,), (0,)), ((), ())), preferred_element_type=jnp.float32
    )


def times_transposed(left, right):
    return lax.dot_general(
        left, right, (((1,), (1,)), ((), ())), preferred_element_type=jnp.float32
    )


def combine(earlier, later):
    return (earlier[0] * later[0], later[0] * earlier[1] + later[1])


def inverse_rms(value):
    return lax.rsqrt(jnp.mean(value * value, axis=-1, keepdims=True) + epsilon)


def sigmoid_slope(raw, sig):
    return sig * (1.0 + raw * (1.0 - sig))


def per_device(
    tokens,
    lengths,
    w_in,
    w_forget,
    w_gate,
    w_out,
    attn_gain,
    mix_gain,
    bound_table,
    ff_gate,
    ff_up,
    ff_down,
    mlp_gain,
    out_grad,
):
    whole = lax.all_gather(tokens, "mp", axis=0, tiled=True)
    mixer = (
        lax.all_gather(w_in, "dp", axis=0, tiled=True),
        lax.all_gather(w_forget, "dp", axis=0, tiled=True),
        lax.all_gather(w_gate, "dp", axis=0, tiled=True),
        lax.all_gather(w_out, "dp", axis=0, tiled=True),
        lax.all_gather(attn_gain, "dp", axis=0, tiled=True),
        lax.all_gather(mix_gain, "dp", axis=0, tiled=True),
        lax.all_gather(bound_table, "dp", axis=1, tiled=True),
    )
    dense = (
        lax.all_gather(ff_gate, "dp", axis=0, tiled=True),
        lax.all_gather(ff_up, "dp", axis=0, tiled=True),
        lax.all_gather(ff_down, "dp", axis=1, tiled=True),
        lax.all_gather(mlp_gain, "dp", axis=0, tiled=True),
    )
    row_count = whole.shape[0]
    half_rows = row_count // lax.axis_size("mp")
    width = whole.shape[1]
    layer_rows = bound_table.shape[0]
    mp_index = lax.axis_index("mp")
    starts = jnp.cumsum(lengths) - lengths
    position = lax.axis_index("dp") * row_count + jnp.arange(row_count, dtype=jnp.int32)
    opening = jnp.any(position[:, None] == starts[None, :], axis=1)
    keep = (1.0 - opening.astype(jnp.float32))[:, None]
    table_f = mixer[6].astype(jnp.float32)
    soft = jax.nn.softmax(table_f, axis=0)
    bound = jnp.sum(soft[1 : LAYER + 1], axis=0)
    attn_g = mixer[4].astype(jnp.float32)
    mix_g = mixer[5].astype(jnp.float32)
    mlp_g = dense[3].astype(jnp.float32)
    tokens_wide = whole.astype(jnp.float32)
    inv_tokens = inverse_rms(tokens_wide)
    tokens_hat = tokens_wide * inv_tokens
    normed = (tokens_hat * attn_g).astype(jnp.bfloat16)
    inner = jnp.dot(normed, mixer[0], preferred_element_type=jnp.float32)
    forget_raw = jnp.dot(normed, mixer[1], preferred_element_type=jnp.float32)
    gate_raw = jnp.dot(normed, mixer[2], preferred_element_type=jnp.float32)
    sig_forget = jax.nn.sigmoid(forget_raw)
    forget = bound + (1.0 - bound) * sig_forget
    sig_inner = jax.nn.sigmoid(inner)
    silu_inner = inner * sig_inner
    drive = silu_inner * (1.0 - forget)
    decay = forget * keep
    decay_all, state_all = lax.associative_scan(combine, (decay, drive), axis=0)
    ones_vec = jnp.ones((width,), jnp.float32)
    zeros_vec = jnp.zeros((width,), jnp.float32)
    carry_in = entering(
        (decay_all[-1], state_all[-1]), "dp", combine, (ones_vec, zeros_vec), False
    )[1]
    states = decay_all * carry_in[None, :] + state_all
    inv_states = inverse_rms(states)
    states_hat = states * inv_states
    sig_gate = jax.nn.sigmoid(gate_raw)
    silu_gate = gate_raw * sig_gate
    mixed_in = (states_hat * mix_g * silu_gate).astype(jnp.bfloat16)
    resid = tokens_wide + jnp.dot(mixed_in, mixer[3], preferred_element_type=jnp.float32)
    inv_resid = inverse_rms(resid)
    resid_hat = resid * inv_resid
    hidden_in = (resid_hat * mlp_g).astype(jnp.bfloat16)
    gate_ff = jnp.dot(hidden_in, dense[0], preferred_element_type=jnp.float32)
    up_ff = jnp.dot(hidden_in, dense[1], preferred_element_type=jnp.float32)
    sig_ff = jax.nn.sigmoid(gate_ff)
    silu_ff = gate_ff * sig_ff
    act = (silu_ff * up_ff).astype(jnp.bfloat16)
    partial_out = jnp.dot(act, dense[2], preferred_element_type=jnp.float32)
    glu_out = lax.psum_scatter(
        partial_out.astype(jnp.bfloat16), "mp", scatter_dimension=0, tiled=True
    ).astype(jnp.float32)
    own_resid = lax.dynamic_slice_in_dim(resid, mp_index * half_rows, half_rows, 0)
    result = (own_resid + glu_out).astype(jnp.bfloat16)
    grad_whole = lax.all_gather(out_grad, "mp", axis=0, tiled=True)
    grad_wide = grad_whole.astype(jnp.float32)
    d_act = times_transposed(grad_whole, dense[2])
    grad_down = contract_rows(act, grad_whole)
    d_gate_ff = (d_act * up_ff * sigmoid_slope(gate_ff, sig_ff)).astype(jnp.bfloat16)
    d_up_ff = (d_act * silu_ff).astype(jnp.bfloat16)
    grad_gate_ff = contract_rows(hidden_in, d_gate_ff)
    grad_up_ff = contract_rows(hidden_in, d_up_ff)
    d_hidden_part = times_transposed(d_gate_ff, dense[0]) + times_transposed(d_up_ff, dense[1])
    d_hidden = lax.psum(d_hidden_part, "mp")
    grad_mlp = jnp.sum(d_hidden * resid_hat, axis=0)
    glu_grads = (
        lax.psum_scatter(grad_gate_ff, "dp", scatter_dimension=0, tiled=True),
        lax.psum_scatter(grad_up_ff, "dp", scatter_dimension=0, tiled=True),
        lax.psum_scatter(grad_down, "dp", scatter_dimension=1, tiled=True),
        lax.psum_scatter(grad_mlp, "dp", scatter_dimension=0, tiled=True),
    )
    scaled_hidden = d_hidden * mlp_g
    d_resid = grad_wide + inv_resid * (
        scaled_hidden - resid_hat * jnp.mean(scaled_hidden * resid_hat, axis=-1, keepdims=True)
    )
    d_mixed = d_resid.astype(jnp.bfloat16)
    grad_out = contract_rows(mixed_in, d_mixed)
    d_mixin = times_transposed(d_mixed, mixer[3])
    grad_mix = jnp.sum(d_mixin * states_hat * silu_gate, axis=0)
    d_gate_raw = (d_mixin * states_hat * mix_g * sigmoid_slope(gate_raw, sig_gate)).astype(
        jnp.bfloat16
    )
    scaled_states = d_mixin * mix_g * silu_gate
    d_states = inv_states * (
        scaled_states - states_hat * jnp.mean(scaled_states * states_hat, axis=-1, keepdims=True)
    )
    decay_next = jnp.concatenate([decay[1:], jnp.ones((1, width), jnp.float32)], axis=0)
    tail_all, adjoint_local = lax.associative_scan(
        combine, (decay_next, d_states), reverse=True, axis=0
    )
    first_decay = decay[0]
    incoming = entering(
        (first_decay * tail_all[0], first_decay * adjoint_local[0]),
        "dp",
        combine,
        (ones_vec, zeros_vec),
        True,
    )[1]
    adjoint = adjoint_local + tail_all * incoming[None, :]
    prev_states = jnp.concatenate([carry_in[None, :], states[:-1]], axis=0)
    d_forget = adjoint * prev_states * keep - adjoint * silu_inner
    d_inner = (adjoint * (1.0 - forget) * sigmoid_slope(inner, sig_inner)).astype(jnp.bfloat16)
    d_forget_raw = (d_forget * (1.0 - bound) * sig_forget * (1.0 - sig_forget)).astype(jnp.bfloat16)
    d_bound = jnp.sum(d_forget * (1.0 - sig_forget), axis=0)
    row_ids = jnp.arange(layer_rows)[:, None]
    member = jnp.logical_and(row_ids >= 1, row_ids <= LAYER).astype(jnp.float32)
    grad_table = soft * (member - bound[None, :]) * d_bound[None, :]
    grad_in = contract_rows(normed, d_inner)
    grad_forget = contract_rows(normed, d_forget_raw)
    grad_gate = contract_rows(normed, d_gate_raw)
    d_normed = (
        times_transposed(d_inner, mixer[0])
        + times_transposed(d_forget_raw, mixer[1])
        + times_transposed(d_gate_raw, mixer[2])
    )
    grad_attn = jnp.sum(d_normed * tokens_hat, axis=0)
    scaled_normed = d_normed * attn_g
    d_tokens = d_resid + inv_tokens * (
        scaled_normed - tokens_hat * jnp.mean(scaled_normed * tokens_hat, axis=-1, keepdims=True)
    )
    token_grad = lax.dynamic_slice_in_dim(d_tokens, mp_index * half_rows, half_rows, 0)
    mixer_grads = (
        lax.psum_scatter(grad_in, "dp", scatter_dimension=0, tiled=True),
        lax.psum_scatter(grad_forget, "dp", scatter_dimension=0, tiled=True),
        lax.psum_scatter(grad_gate, "dp", scatter_dimension=0, tiled=True),
        lax.psum_scatter(grad_out, "dp", scatter_dimension=0, tiled=True),
        lax.psum_scatter(grad_attn, "dp", scatter_dimension=0, tiled=True),
        lax.psum_scatter(grad_mix, "dp", scatter_dimension=0, tiled=True),
        lax.psum_scatter(grad_table, "dp", scatter_dimension=1, tiled=True),
    )
    return (
        result,
        token_grad,
        mixer_grads[0],
        mixer_grads[1],
        mixer_grads[2],
        mixer_grads[3],
        mixer_grads[4],
        mixer_grads[5],
        mixer_grads[6],
        glu_grads[0],
        glu_grads[1],
        glu_grads[2],
        glu_grads[3],
    )


def solution(mesh):
    return jax.shard_map(
        per_device,
        mesh=mesh,
        in_specs=(
            P(("dp", "mp"), None),
            P(),
            P("dp", None),
            P("dp", None),
            P("dp", None),
            P("dp", None),
            P("dp"),
            P("dp"),
            P(None, "dp"),
            P("dp", "mp"),
            P("dp", "mp"),
            P("mp", "dp"),
            P("dp"),
            P(("dp", "mp"), None),
        ),
        out_specs=(
            P(("dp", "mp"), None),
            P(("dp", "mp"), None),
            P("dp", None),
            P("dp", None),
            P("dp", None),
            P("dp", None),
            P("dp"),
            P("dp"),
            P(None, "dp"),
            P("dp", "mp"),
            P("dp", "mp"),
            P("mp", "dp"),
            P("dp"),
        ),
        check_vma=False,
    )
```

profile of v0, /device:TPU:0, one launch (start us, length us, event | category | flops | bytes accessed | tf_op | source)
XLA Modules:
  0.0 2432.1 jit_solution(4686550156488616628)
XLA Ops:
  11.9 10.2 all_gather.53
  22.3 22.1 all-gather
  44.5 18.7 all_gather.54
  66.2 18.7 all-gather.3
  85.5 17.7 all-gather.4
  103.8 10.7 all_gather.67
  119.3 44.6 %all-gather.15.cloned.1.call-done = bf16[2048,2048]{1,0:T(8,128)(2,1)} async-done(((bf16[128,2048]{1,0:T(8,128)(2,1)}), bf16[2048,2048]{1,0:T(8,128)(2,1)}) %all-gather.15.cloned.1.call-update) | async-done | bytes 8388624 | tf_op jit(solution)/shard_map/all_gather | solution.py:70
  163.9 6.4 fusion.9
  241.0 19.5 all-gather.2
  270.6 18.3 all-gather.1
  298.4 17.0 all-gather.21.cloned.1.call-done
  320.3 90.0 %all-gather.23.cloned.1.call-done = bf16[2048,2816]{1,0:T(8,128)(2,1)} async-done(((bf16[128,2816]{1,0:T(8,128)(2,1)}), bf16[2048,2816]{1,0:T(8,128)(2,1)}) %all-gather.23.cloned.1.call-update) | async-done | bytes 11534352 | tf_op jit(solution)/shard_map/all_gather | solution.py:78
  410.4 7.1 fusion.58
  417.4 87.6 %all-gather.25.cloned.1.call-done = bf16[2048,2816]{1,0:T(8,128)(2,1)} async-done(((bf16[128,2816]{1,0:T(8,128)(2,1)}), bf16[2048,2816]{1,0:T(8,128)(2,1)}) %all-gather.25.cloned.1.call-update) | async-done | bytes 11534352 | tf_op jit(solution)/shard_map/all_gather | solution.py:79
  505.0 7.0 fusion.59
  512.1 90.7 %all-gather.27.cloned.1.call-done = bf16[2816,2048]{1,0:T(8,128)(2,1)} async-done(((bf16[2816,128]{1,0:T(8,128)(2,1)}), bf16[2816,2048]{1,0:T(8,128)(2,1)}) %all-gather.27.cloned.1.call-update) | async-done | bytes 11534352 | tf_op jit(solution)/shard_map/all_gather | solution.py:80
  602.8 10.3 multiply_convert_fusion
  613.9 8.2 fusion.60
  640.0 8.3 slice.514
  648.2 8.3 slice.521
  656.5 8.3 slice.512
  664.8 7.0 convolution_convert_fusion
  676.7 8.3 multiply_reduce_fusion.2
  692.9 8.2 slice.516
  701.1 8.2 slice.518
  837.2 8.3 slice.566
  867.1 19.5 all-gather.5
  891.5 18.4 all-gather.6
  914.8 13.9 while.29
  928.7 8.9 rev.15
  937.6 8.9 rev.14
  954.0 9.0 fusion.38
  964.0 8.4 fusion.39
  973.6 9.2 fusion.15
  982.9 9.2 fusion.37
  992.4 10.6 fusion.62
  1003.0 10.5 fusion.63
  1014.5 14.7 fusion.64
  1031.2 7.9 fusion.61
  1039.1 6.5 convolution_add_fusion.2
  1049.9 62.9 %all-reduce.61 = (f32[2048]{0:T(1024)S(1)}, f32[2048]{0:T(1024)S(1)}, f32[2048]{0:T(1024)S(1)}) all-reduce(f32[2048]{0:T(1024)S(1)} %get-tuple-element.243, f32[2048]{0:T(1024)S(1)} %copy-done.36, f32[2048]{0:T(1024)S(1)} %copy-done.28), channel_id=7, replica_groups=mesh['dp'=16,'mp'=2] {'dp'}, use_global_device_ids=true, to_apply=%region_22.23.clone | all-reduce | flops 6144 | bytes 49152
  1118.5 68.8 %reduce-scatter.14.cloned.1.call-done = f32[128,2048]{1,0:T(8,128)} async-done(((f32[2048,2048]{1,0:T(8,128)}), f32[128,2048]{1,0:T(8,128)}) %reduce-scatter.14.cloned.1.call-update) | async-done | bytes 1048592 | tf_op jit(solution)/shard_map/reduce_scatter | solution.py:207
  1187.3 182.2 %reduce-scatter.12.cloned.1.call-done = f32[128,2048]{1,0:T(8,128)} async-done(((f32[2048,2048]{1,0:T(8,128)}), f32[128,2048]{1,0:T(8,128)}) %reduce-scatter.12.cloned.1.call-update) | async-done | bytes 1048592 | tf_op jit(solution)/shard_map/reduce_scatter | solution.py:206
  1369.4 182.3 %reduce-scatter.18.cloned.1.call-done = f32[128,2048]{1,0:T(8,128)} async-done(((f32[2048,2048]{1,0:T(8,128)}), f32[128,2048]{1,0:T(8,128)}) %reduce-scatter.18.cloned.1.call-update) | async-done | bytes 1048592 | tf_op jit(solution)/shard_map/reduce_scatter | solution.py:209
  1551.7 182.1 %reduce-scatter.16.cloned.1.call-done = f32[128,2048]{1,0:T(8,128)} async-done(((f32[2048,2048]{1,0:T(8,128)}), f32[128,2048]{1,0:T(8,128)}) %reduce-scatter.16.cloned.1.call-update) | async-done | bytes 1048592 | tf_op jit(solution)/shard_map/reduce_scatter | solution.py:208
  1733.9 230.4 %reduce-scatter.22.cloned.1.call-done = f32[128,2816]{1,0:T(8,128)} async-done(((f32[2048,2816]{1,0:T(8,128)}), f32[128,2816]{1,0:T(8,128)}) %reduce-scatter.22.cloned.1.call-update) | async-done | bytes 1441808 | tf_op jit(solution)/shard_map/reduce_scatter | solution.py:150
  1964.3 230.5 %reduce-scatter.24.cloned.1.call-done = f32[128,2816]{1,0:T(8,128)} async-done(((f32[2048,2816]{1,0:T(8,128)}), f32[128,2816]{1,0:T(8,128)}) %reduce-scatter.24.cloned.1.call-update) | async-done | bytes 1441808 | tf_op jit(solution)/shard_map/reduce_scatter | solution.py:151
  2194.8 230.5 %reduce-scatter.26.cloned.1.call-done = f32[2816,128]{1,0:T(8,128)} async-done(((f32[2816,2048]{1,0:T(8,128)}), f32[2816,128]{1,0:T(8,128)}) %reduce-scatter.26.cloned.1.call-update) | async-done | bytes 1441808 | tf_op jit(solution)/shard_map/reduce_scatter | solution.py:152
  (457 shorter events, 335.1 us)
Async XLA Ops:
  7.2 107.3 %all-gather.17.cloned.1.call-start = ((), (), s32[]{:S(2)}) async-start(), calls=%async_computation.10 | async-start | bytes 8912896 | tf_op jit(solution)/shard_map/all_gather | solution.py:69
  7.9 156.0 %all-gather.15.cloned.1.call-start = ((), (), s32[]{:S(2)}) async-start(), calls=%async_computation.9 | async-start | bytes 8912896 | tf_op jit(solution)/shard_map/all_gather | solution.py:70
  8.7 283.7 %all-gather.19.cloned.1.call-start = ((), (), s32[]{:S(2)}) async-start(), calls=%async_computation.11 | async-start | bytes 8912896 | tf_op jit(solution)/shard_map/all_gather | solution.py:71
  9.4 306.0 %all-gather.21.cloned.1.call-start = ((), (), s32[]{:S(2)}) async-start(), calls=%async_computation.12 | async-start | bytes 8912896 | tf_op jit(solution)/shard_map/all_gather | solution.py:72
  10.0 400.4 %all-gather.23.cloned.1.call-start = ((), (), s32[]{:S(2)}) async-start(), calls=%async_computation.13 | async-start | bytes 12255232 | tf_op jit(solution)/shard_map/all_gather | solution.py:78
  10.6 494.5 %all-gather.25.cloned.1.call-start = ((), (), s32[]{:S(2)}) async-start(), calls=%async_computation.14 | async-start | bytes 12255232 | tf_op jit(solution)/shard_map/all_gather | solution.py:79
  11.1 591.6 %all-gather.27.cloned.1.call-start = ((), (), s32[]{:S(2)}) async-start(), calls=%async_computation.15 | async-start | bytes 12255232 | tf_op jit(solution)/shard_map/all_gather | solution.py:80
  11.9 660.0 %all-reduce.64.cloned.1.call-start = ((), (), s32[]{:S(2)}) async-start(), calls=%async_computation.17 | async-start | bytes 2097152 | tf_op jit(solution)/shard_map/psum | solution.py:147
  22.3 141.6 %copy-start.25 = (f32[128]{0:T(128)}, f32[128]{0:T(128)S(1)}, u32[]{:S(2)}) copy-start(f32[128]{0:T(128)S(1)} %add_rsqrt_fusion.2) | copy-start | bytes 1540
  64.5 99.4 %copy-start.18 = (f32[2048]{0:T(1024)}, f32[2048]{0:T(1024)S(1)}, u32[]{:S(2)}) copy-start(f32[2048]{0:T(1024)S(1)} %slice_reduce_fusion) | copy-start | bytes 24580
  64.5 99.4 %copy-start.22 = (f32[2048]{0:T(1024)}, f32[2048]{0:T(1024)S(1)}, u32[]{:S(2)}) copy-start(f32[2048]{0:T(1024)S(1)} %broadcast_subtract_fusion) | copy-start | bytes 24580
  66.2 97.7 %copy-start.37 = (f32[128]{0:T(128)}, f32[128]{0:T(128)S(1)}, u32[]{:S(2)}) copy-start(f32[128]{0:T(128)S(1)} %convert_subtract_fusion) | copy-start | bytes 1540
  119.3 51.0 %copy-start.10 = (f32[128,2048]{1,0:T(8,128)}, f32[128,2048]{1,0:T(8,128)S(1)}, u32[]{:S(2)}) copy-start(f32[128,2048]{1,0:T(8,128)S(1)} %fusion.41) | copy-start | bytes 3145732
  170.3 51.7 %copy-start = (f32[128,2048]{1,0:T(8,128)}, f32[128,2048]{1,0:T(8,128)S(1)}, u32[]{:S(2)}) copy-start(f32[128,2048]{1,0:T(8,128)S(1)} %get-tuple-element.282) | copy-start | bytes 3145732
  213.5 17.0 copy-start.35
  215.1 15.7 copy-start.16
  215.7 15.2 copy-start.32
  231.0 29.5 %copy-start.30 = (f32[1,2048]{1,0:T(1,128)S(1)}, f32[1,2048]{1,0:T(1,128)}, u32[]{:S(2)}) copy-start(f32[1,2048]{1,0:T(1,128)} %slice.583) | copy-start | bytes 24580
  234.9 57.5 %copy-start.26 = (f32[128]{0:T(128)S(1)}, f32[128]{0:T(128)}, u32[]{:S(2)}) copy-start(f32[128]{0:T(128)} %copy-done.25) | copy-start | bytes 1540
  234.9 57.5 %copy-start.29 = (f32[16,1,128]{2,1,0:T(1,128)S(1)}, f32[16,1,128]{2,1,0:T(1,128)}, u32[]{:S(2)}) copy-start(f32[16,1,128]{2,1,0:T(1,128)} %convert_element_type.94) | copy-start | bytes 24580
  237.1 53.0 %copy-start.8 = (f32[128,2048]{1,0:T(8,128)S(1)}, f32[128,2048]{1,0:T(8,128)}, u32[]{:S(2)}) copy-start(f32[128,2048]{1,0:T(8,128)} %pad.201) | copy-start | bytes 3145732
  240.0 50.1 %copy-start.9 = (f32[128,2048]{1,0:T(8,128)}, f32[128,2048]{1,0:T(8,128)S(1)}, u32[]{:S(2)}) copy-start(f32[128,2048]{1,0:T(8,128)S(1)} %pad.200) | copy-start | bytes 3145732
  298.4 21.8 copy-start.11
  298.4 21.8 copy-start.17
  602.8 19.4 slice-start
  602.8 19.4 slice-start.1
  613.1 9.1 copy-start.12
  613.9 8.2 slice-start.2
  627.2 487.4 %reduce-scatter.10.cloned.1.call-start = ((), (), s32[]{:S(2)}) async-start(), calls=%async_computation.16 | async-start | bytes 786432 | tf_op jit(solution)/shard_map/reduce_scatter | solution.py:133
  671.8 446.7 %reduce-scatter.20.cloned.1.call-start = ((), (), s32[]{:S(2)}) async-start(), calls=%async_computation.22 | async-start | bytes 208896 | tf_op jit(solution)/shard_map/reduce_scatter | solution.py:212
  675.7 9.2 copy-start.15
  777.4 36.8 %copy-start.34 = (f32[1,2048]{1,0:T(1,128)S(1)}, f32[1,2048]{1,0:T(1,128)}, u32[]{:S(2)}) copy-start(f32[1,2048]{1,0:T(1,128)} %slice.653) | copy-start | bytes 24580
  777.4 47.8 %copy-start.33 = (f32[1,2048]{1,0:T(1,128)S(1)}, f32[1,2048]{1,0:T(1,128)}, u32[]{:S(2)}) copy-start(f32[1,2048]{1,0:T(1,128)} %slice.631) | copy-start | bytes 24580
  849.1 97.3 %copy-start.19 = (f32[2048]{0:T(1024)S(1)}, f32[2048]{0:T(1024)}, u32[]{:S(2)}) copy-start(f32[2048]{0:T(1024)} %copy-done.18) | copy-start | bytes 24580
  849.1 97.3 %copy-start.23 = (f32[2048]{0:T(1024)S(1)}, f32[2048]{0:T(1024)}, u32[]{:S(2)}) copy-start(f32[2048]{0:T(1024)} %copy-done.22) | copy-start | bytes 24580
  862.9 87.8 %copy-start.21 = (f32[2048]{0:T(1024)S(1)}, f32[2048]{0:T(1024)}, u32[]{:S(2)}) copy-start(f32[2048]{0:T(1024)} %copy-done.20) | copy-start | bytes 24580
  953.9 9.1 copy-start.6
  953.9 233.4 %reduce-scatter.14.cloned.1.call-start = ((), (), s32[]{:S(2)}) async-start(), calls=%async_computation.19 | async-start | bytes 17825792 | tf_op jit(solution)/shard_map/reduce_scatter | solution.py:207
  963.0 406.5 %reduce-scatter.12.cloned.1.call-start = ((), (), s32[]{:S(2)}) async-start(), calls=%async_computation.18 | async-start | bytes 17825792 | tf_op jit(solution)/shard_map/reduce_scatter | solution.py:206
  972.4 579.3 %reduce-scatter.18.cloned.1.call-start = ((), (), s32[]{:S(2)}) async-start(), calls=%async_computation.21 | async-start | bytes 17825792 | tf_op jit(solution)/shard_map/reduce_scatter | solution.py:209
  982.9 751.0 %reduce-scatter.16.cloned.1.call-start = ((), (), s32[]{:S(2)}) async-start(), calls=%async_computation.20 | async-start | bytes 17825792 | tf_op jit(solution)/shard_map/reduce_scatter | solution.py:208
  992.2 972.1 %reduce-scatter.22.cloned.1.call-start = ((), (), s32[]{:S(2)}) async-start(), calls=%async_computation.23 | async-start | bytes 24510464 | tf_op jit(solution)/shard_map/reduce_scatter | solution.py:150
  1003.0 1191.9 %reduce-scatter.24.cloned.1.call-start = ((), (), s32[]{:S(2)}) async-start(), calls=%async_computation.24 | async-start | bytes 24510464 | tf_op jit(solution)/shard_map/reduce_scatter | solution.py:151
  1013.5 1411.8 %reduce-scatter.26.cloned.1.call-start = ((), (), s32[]{:S(2)}) async-start(), calls=%async_computation.25 | async-start | bytes 24510464 | tf_op jit(solution)/shard_map/reduce_scatter | solution.py:152
  1031.2 7.9 copy-start.7
  1031.2 14.4 slice-start.3
  1031.2 14.4 copy-start.14
  1039.1 6.5 slice-start.4
  (13 other events, 24.7 us)
Sparse Core Ops, SparseCore 0:
  10.2 77.9 all-gather.16
  90.3 73.4 all-gather.14
  166.0 73.1 all-gather.18
  241.2 74.0 all-gather.20
  317.5 92.8 all-gather.22
  412.5 92.4 all-gather.24
  507.2 95.5 all-gather.26
  627.3 38.2 all-reduce.63
  671.9 12.7 reduce-scatter.9
  954.0 51.4 reduce-scatter.19
  1010.2 177.0 reduce-scatter.13
  1191.8 177.5 reduce-scatter.11
  1374.1 177.5 reduce-scatter.17
  1556.3 177.5 reduce-scatter.15
  1738.4 225.8 reduce-scatter.21
  1968.8 225.9 reduce-scatter.23
  2199.3 225.9 reduce-scatter.25
where the time goes:
time: 2450 us; the launch traced here: 2430 us
  waiting for transfers between devices  1640 us (67%)
  local copies, waits for them, and re-layouts  276 us (11%)
  blocking collectives  237 us (10%)
  matrix products  165 us (7%)
  other arithmetic  95 us (4%)
    reduce_scatter x1, waiting for transfers between devices, per_device(): lax.psum_scatter(grad_up_ff, 'dp', scatter_dimension=0, tiled=True)  231 us
    reduce_scatter x1, waiting for transfers between devices, per_device(): lax.psum_scatter(grad_down, 'dp', scatter_dimension=1, tiled=True)  231 us
    reduce_scatter x1, waiting for transfers between devices, per_device(): lax.psum_scatter(grad_gate_ff, 'dp', scatter_dimension=0, tiled=True)  230 us
    reduce_scatter x1, waiting for transfers between devices, per_device(): lax.psum_scatter(grad_out, 'dp', scatter_dimension=0, tiled=True)  182 us
    reduce_scatter x1, waiting for transfers between devices, per_device(): lax.psum_scatter(grad_in, 'dp', scatter_dimension=0, tiled=True)  182 us
    reduce_scatter x1, waiting for transfers between devices, per_device(): lax.psum_scatter(grad_gate, 'dp', scatter_dimension=0, tiled=True)  182 us
    slice x49, local copies, waits for them, and re-layouts, per_device(): lax.associative_scan(combine, (decay_next, d_states), reverse=True, axis=0)  121 us
    all_gather x1, waiting for transfers between devices, per_device(): lax.all_gather(ff_down, 'dp', axis=1, tiled=True)  90.7 us
  transfers between devices with their start and end apart: 17, of which 12 were waited for; matrix products, arithmetic and copies ran while one was open for 21% of the time, Pallas kernels for 0%

commit v1 on v0

--- a/solution.py
+++ b/solution.py
@@ -74,8 +74,27 @@
         lax.all_gather(mix_gain, "dp", axis=0, tiled=True),
         lax.all_gather(bound_table, "dp", axis=1, tiled=True),
     )
+
+    def lift_steps_all(shard_in):
+        ndev = lax.axis_size("dp")
+        heap = []
+        for j in tuple(range(ndev)):
+            heap.append((j, (j + 1) % ndev))
+        ledger = []
+        for j in tuple(range(ndev)):
+            ledger.append((j, (j - 1) % ndev))
+        block_out, b_now = ([shard_in], [shard_in])
+        for _ in range(ndev // 2):
+            block_out.append(lax.ppermute(block_out[-1], axis_name="dp", perm=heap))
+        for _ in [*range((ndev - 1) // 2)]:
+            v1 = lax.ppermute(b_now[-1], axis_name="dp", perm=ledger)
+            b_now.append(v1)
+        a_now = jnp.concatenate([*block_out[::-1], *b_now[1:]], 0)
+        back = jnp.roll(a_now, (lax.axis_index("dp") - ndev // 2) * shard_in.shape[0], 0)
+        return back
+
     dense = (
-        lax.all_gather(ff_gate, "dp", axis=0, tiled=True),
+        lift_steps_all(ff_gate),
         lax.all_gather(ff_up, "dp", axis=0, tiled=True),
         lax.all_gather(ff_down, "dp", axis=1, tiled=True),
         lax.all_gather(mlp_gain, "dp", axis=0, tiled=True),

time: 2450 us -> 2400 us (0.980)
  waiting for transfers between devices: 1640 us -> 1490 us
  local copies, waits for them, and re-layouts: 276 us -> 318 us
  starting transfers between devices: 0.85 us -> 26.8 us
    all_gather x1 -> x0, waiting for transfers between devices: 90 us -> none  [per_device(): lax.all_gather(ff_gate, 'dp', axis=0, tiled=True)]
    ppermute x0 -> x15, waiting for transfers between devices: none -> 89 us  [the longest x8 86.1 us: lift_steps_all(): block_out.append(lax.ppermute(block_out[-1], axis_name='dp', perm=heap))]
    all_gather x1, waiting for transfers between devices: 87.6 us -> 5.88 us  [per_device(): lax.all_gather(ff_up, 'dp', axis=0, tiled=True)]
    unnamed x96 -> x139, local copies, waits for them, and re-layouts: 9.18 us -> 57 us
    all_gather x1, waiting for transfers between devices: 44.6 us -> 0.02 us  [per_device(): lax.all_gather(w_forget, 'dp', axis=0, tiled=True)]
    ppermute x0 -> x15, starting transfers between devices: none -> 25.9 us  [the longest x7 25.4 us: lift_steps_all(): v1 = lax.ppermute(b_now[-1], axis_name='dp', perm=ledger)]
  transfers between devices with their start and end apart: 17 -> 31, of which waited for: 12 -> 15; matrix products, arithmetic and copies ran while one was open for 21% -> 23% of each run, Pallas kernels for 0% -> 0%
where the time goes in v1:
time: 2400 us; the launch traced here: 2380 us
  waiting for transfers between devices  1490 us (62%)
  local copies, waits for them, and re-layouts  318 us (13%)
  blocking collectives  260 us (11%)
  matrix products  170 us (7%)
  other arithmetic  97.2 us (4%)
  starting transfers between devices  26.8 us (1%)
    reduce_scatter x1, waiting for transfers between devices, per_device(): lax.psum_scatter(grad_down, 'dp', scatter_dimension=1, tiled=True)  231 us
    reduce_scatter x1, waiting for transfers between devices, per_device(): lax.psum_scatter(grad_gate_ff, 'dp', scatter_dimension=0, tiled=True)  230 us
    reduce_scatter x1, waiting for transfers between devices, per_device(): lax.psum_scatter(grad_up_ff, 'dp', scatter_dimension=0, tiled=True)  230 us
    reduce_scatter x1, waiting for transfers between devices, per_device(): lax.psum_scatter(grad_in, 'dp', scatter_dimension=0, tiled=True)  182 us
    reduce_scatter x1, waiting for transfers between devices, per_device(): lax.psum_scatter(grad_gate, 'dp', scatter_dimension=0, tiled=True)  182 us
    reduce_scatter x1, waiting for transfers between devices, per_device(): lax.psum_scatter(grad_out, 'dp', scatter_dimension=0, tiled=True)  182 us
    slice x49, local copies, waits for them, and re-layouts, per_device(): lax.associative_scan(combine, (decay_next, d_states), reverse=True, axis=0)  108 us
    all_gather x1, waiting for transfers between devices, per_device(): lax.all_gather(ff_down, 'dp', axis=1, tiled=True)  90.6 us
  transfers between devices with their start and end apart: 31, of which 15 were waited for; matrix products, arithmetic and copies ran while one was open for 23% of the time, Pallas kernels for 0%

profile of v1, /device:TPU:0, one launch (start us, length us, event | category | flops | bytes accessed | tf_op | source)
XLA Modules:
  0.0 2383.4 jit_solution(7033820559271498536)
XLA Ops:
  11.1 14.3 collective-permute-done
  29.8 21.5 collective-permute-done.1
  55.8 23.6 collective-permute-done.2
  84.8 10.9 collective-permute-done.3
  100.2 15.7 collective-permute-done.4
  115.9 24.5 %all_gather.51 = bf16[24,2048]{1,0:T(8,128)(2,1)S(1)} all-gather(bf16[24,128]{1,0:T(8,128)(2,1)} %param.26), channel_id=1, replica_groups=mesh['dp'=16,'mp'=2] {'dp'}, dimensions={1}, use_global_device_ids=true | all-gather | bytes 104448 | tf_op jit(solution)/shard_map/all_gather | solution.py:75
  144.9 9.3 all_gather.50
  154.2 10.2 all_gather.63
  172.2 40.4 %all-gather = bf16[16,1,128]{2,1,0:T(2,128)(2,1)S(1)} all-gather(bf16[1,1,128]{2,1,0:T(2,128)(2,1)} %bitcast.100), channel_id=1, replica_groups=mesh['dp'=16,'mp'=2] {'dp'}, dimensions={0}, use_global_device_ids=true | all-gather | bytes 4352 | tf_op jit(solution)/shard_map/all_gather | solution.py:73
  212.7 17.5 all-gather.3
  230.8 18.9 all-gather.4
  307.5 6.7 fusion.16
  411.2 19.6 all-gather.2
  437.7 18.5 all-gather.1
  478.7 7.1 fusion.67
  485.7 90.6 %all-gather.24.cloned.1.call-done = bf16[2816,2048]{1,0:T(8,128)(2,1)} async-done(((bf16[2816,128]{1,0:T(8,128)(2,1)}), bf16[2816,2048]{1,0:T(8,128)(2,1)}) %all-gather.24.cloned.1.call-update) | async-done | bytes 11534352 | tf_op jit(solution)/shard_map/all_gather | solution.py:99
  576.3 8.4 fusion.68
  584.7 8.2 multiply_convert_fusion.1
  596.8 9.3 fusion.5
  617.8 8.3 slice.514
  626.1 8.3 slice.521
  639.5 7.0 convolution_convert_fusion
  651.4 8.4 multiply_reduce_fusion.2
  667.8 8.3 slice.516
  787.8 8.3 slice.566
  818.3 19.5 all-gather.5
  842.7 18.2 all-gather.6
  865.8 13.9 while.29
  879.8 8.9 rev.15
  888.6 8.9 rev.14
  905.0 9.0 fusion.47
  914.1 9.4 fusion.48
  923.6 9.2 fusion.22
  932.9 9.3 fusion.46
  942.5 10.5 fusion.71
  953.0 10.5 fusion.72
  963.7 14.7 fusion.73
  979.8 8.0 fusion.70
  987.8 6.5 convolution_add_fusion.1
  994.4 8.4 multiply_reduce_fusion.3
  1002.7 63.2 %all-reduce.61 = (f32[2048]{0:T(1024)S(1)}, f32[2048]{0:T(1024)S(1)}, f32[2048]{0:T(1024)S(1)}) all-reduce(f32[2048]{0:T(1024)S(1)} %get-tuple-element.243, f32[2048]{0:T(1024)S(1)} %copy-done.44, f32[2048]{0:T(1024)S(1)} %copy-done.40), channel_id=7, replica_groups=mesh['dp'=16,'mp'=2] {'dp'}, use_global_device_ids=true, to_apply=%region_22.23.clone | all-reduce | flops 6144 | bytes 49152
  1071.6 66.7 %reduce-scatter.14.cloned.1.call-done = f32[128,2048]{1,0:T(8,128)} async-done(((f32[2048,2048]{1,0:T(8,128)}), f32[128,2048]{1,0:T(8,128)}) %reduce-scatter.14.cloned.1.call-update) | async-done | bytes 1048592 | tf_op jit(solution)/shard_map/reduce_scatter | solution.py:226
  1138.3 182.3 %reduce-scatter.12.cloned.1.call-done = f32[128,2048]{1,0:T(8,128)} async-done(((f32[2048,2048]{1,0:T(8,128)}), f32[128,2048]{1,0:T(8,128)}) %reduce-scatter.12.cloned.1.call-update) | async-done | bytes 1048592 | tf_op jit(solution)/shard_map/reduce_scatter | solution.py:225
  1320.7 182.2 %reduce-scatter.18.cloned.1.call-done = f32[128,2048]{1,0:T(8,128)} async-done(((f32[2048,2048]{1,0:T(8,128)}), f32[128,2048]{1,0:T(8,128)}) %reduce-scatter.18.cloned.1.call-update) | async-done | bytes 1048592 | tf_op jit(solution)/shard_map/reduce_scatter | solution.py:228
  1502.8 182.3 %reduce-scatter.16.cloned.1.call-done = f32[128,2048]{1,0:T(8,128)} async-done(((f32[2048,2048]{1,0:T(8,128)}), f32[128,2048]{1,0:T(8,128)}) %reduce-scatter.16.cloned.1.call-update) | async-done | bytes 1048592 | tf_op jit(solution)/shard_map/reduce_scatter | solution.py:227
  1685.1 230.4 %reduce-scatter.22.cloned.1.call-done = f32[128,2816]{1,0:T(8,128)} async-done(((f32[2048,2816]{1,0:T(8,128)}), f32[128,2816]{1,0:T(8,128)}) %reduce-scatter.22.cloned.1.call-update) | async-done | bytes 1441808 | tf_op jit(solution)/shard_map/reduce_scatter | solution.py:169
  1915.5 230.4 %reduce-scatter.24.cloned.1.call-done = f32[128,2816]{1,0:T(8,128)} async-done(((f32[2048,2816]{1,0:T(8,128)}), f32[128,2816]{1,0:T(8,128)}) %reduce-scatter.24.cloned.1.call-update) | async-done | bytes 1441808 | tf_op jit(solution)/shard_map/reduce_scatter | solution.py:170
  2145.9 230.6 %reduce-scatter.26.cloned.1.call-done = f32[2816,128]{1,0:T(8,128)} async-done(((f32[2816,2048]{1,0:T(8,128)}), f32[2816,128]{1,0:T(8,128)}) %reduce-scatter.26.cloned.1.call-update) | async-done | bytes 1441808 | tf_op jit(solution)/shard_map/reduce_scatter | solution.py:171
  (527 shorter events, 424.1 us)
Async XLA Ops:
  7.2 283.6 %copy-start.19 = (bf16[128,2816]{1,0:T(8,128)(2,1)S(1)}, bf16[128,2816]{1,0:T(8,128)(2,1)}, u32[]{:S(2)}) copy-start(bf16[128,2816]{1,0:T(8,128)(2,1)} %param.27) | copy-start | bytes 2162692
  7.2 295.4 %all-gather.16.cloned.1.call-start = ((), (), s32[]{:S(2)}) async-start(), calls=%async_computation.10 | async-start | bytes 8912896 | tf_op jit(solution)/shard_map/all_gather | solution.py:69
  7.9 299.5 %all-gather.14.cloned.1.call-start = ((), (), s32[]{:S(2)}) async-start(), calls=%async_computation.9 | async-start | bytes 8912896 | tf_op jit(solution)/shard_map/all_gather | solution.py:70
  8.7 451.7 %all-gather.18.cloned.1.call-start = ((), (), s32[]{:S(2)}) async-start(), calls=%async_computation.11 | async-start | bytes 8912896 | tf_op jit(solution)/shard_map/all_gather | solution.py:71
  9.4 457.2 %all-gather.20.cloned.1.call-start = ((), (), s32[]{:S(2)}) async-start(), calls=%async_computation.12 | async-start | bytes 8912896 | tf_op jit(solution)/shard_map/all_gather | solution.py:72
  10.0 468.7 %all-gather.22.cloned.1.call-start = ((), (), s32[]{:S(2)}) async-start(), calls=%async_computation.13 | async-start | bytes 12255232 | tf_op jit(solution)/shard_map/all_gather | solution.py:98
  10.6 565.8 %all-gather.24.cloned.1.call-start = ((), (), s32[]{:S(2)}) async-start(), calls=%async_computation.14 | async-start | bytes 12255232 | tf_op jit(solution)/shard_map/all_gather | solution.py:99
  10.6 14.8 collective-permute-start
  25.4 26.0 %collective-permute-start.1 = (bf16[128,2816]{1,0:T(8,128)(2,1)S(1)}, bf16[128,2816]{1,0:T(8,128)(2,1)S(1)}, u32[]{:S(2)}, u32[]{:S(2)}) collective-permute-start(bf16[128,2816]{1,0:T(8,128)(2,1)S(1)} %collective-permute-done), channel_id=1, source_target_pairs={{0,2},{2,4},{4,6},{6,8},{8,10},{10,12},{12,14},{14,16},{16,18},{18... | collective-permute-start | bytes 2162696 | tf_op jit(solution)/shard_map/ppermute | solution.py:88
  25.4 26.0 %collective-permute-start.8 = (bf16[128,2816]{1,0:T(8,128)(2,1)}, bf16[128,2816]{1,0:T(8,128)(2,1)S(1)}, u32[]{:S(2)}, u32[]{:S(2)}) collective-permute-start(bf16[128,2816]{1,0:T(8,128)(2,1)} %param.27), channel_id=1, source_target_pairs={{0,30},{2,0},{4,2},{6,4},{8,6},{10,8},{12,10},{14,12},{16,14},{18,... | collective-permute-start | bytes 2162696 | tf_op jit(solution)/shard_map/ppermute | solution.py:90
  51.4 28.1 %collective-permute-start.2 = (bf16[128,2816]{1,0:T(8,128)(2,1)S(1)}, bf16[128,2816]{1,0:T(8,128)(2,1)S(1)}, u32[]{:S(2)}, u32[]{:S(2)}) collective-permute-start(bf16[128,2816]{1,0:T(8,128)(2,1)S(1)} %collective-permute-done.1), channel_id=1, source_target_pairs={{0,2},{2,4},{4,6},{6,8},{8,10},{10,12},{12,14},{14,16},{16,18},{18... | collective-permute-start | bytes 2162696 | tf_op jit(solution)/shard_map/ppermute | solution.py:88
  51.4 28.1 %collective-permute-start.9 = (bf16[128,2816]{1,0:T(8,128)(2,1)S(1)}, bf16[128,2816]{1,0:T(8,128)(2,1)S(1)}, u32[]{:S(2)}, u32[]{:S(2)}) collective-permute-start(bf16[128,2816]{1,0:T(8,128)(2,1)S(1)} %collective-permute-done.8), channel_id=1, source_target_pairs={{0,30},{2,0},{4,2},{6,4},{8,6},{10,8},{12,10},{14,12},{16,14},{18,... | collective-permute-start | bytes 2162696 | tf_op jit(solution)/shard_map/ppermute | solution.py:90
  79.5 16.2 collective-permute-start.3
  80.4 15.4 collective-permute-start.10
  95.7 20.1 collective-permute-start.4
  95.7 44.8 %collective-permute-start.11 = (bf16[128,2816]{1,0:T(8,128)(2,1)}, bf16[128,2816]{1,0:T(8,128)(2,1)}, u32[]{:S(2)}, u32[]{:S(2)}) collective-permute-start(bf16[128,2816]{1,0:T(8,128)(2,1)} %collective-permute-done.10), channel_id=1, source_target_pairs={{0,30},{2,0},{4,2},{6,4},{8,6},{10,8},{12,10},{14,12},{16,14},{18,... | collective-permute-start | bytes 2162696 | tf_op jit(solution)/shard_map/ppermute | solution.py:90
  115.8 27.4 %collective-permute-start.5 = (bf16[128,2816]{1,0:T(8,128)(2,1)}, bf16[128,2816]{1,0:T(8,128)(2,1)}, u32[]{:S(2)}, u32[]{:S(2)}) collective-permute-start(bf16[128,2816]{1,0:T(8,128)(2,1)} %collective-permute-done.4), channel_id=1, source_target_pairs={{0,2},{2,4},{4,6},{6,8},{8,10},{10,12},{12,14},{14,16},{16,18},{18... | collective-permute-start | bytes 2162696 | tf_op jit(solution)/shard_map/ppermute | solution.py:88
  115.9 530.7 %all-reduce.64.cloned.1.call-start = ((), (), s32[]{:S(2)}) async-start(), calls=%async_computation.16 | async-start | bytes 2097152 | tf_op jit(solution)/shard_map/psum | solution.py:166
  140.6 26.9 %collective-permute-start.12 = (bf16[128,2816]{1,0:T(8,128)(2,1)}, bf16[128,2816]{1,0:T(8,128)(2,1)}, u32[]{:S(2)}, u32[]{:S(2)}) collective-permute-start(bf16[128,2816]{1,0:T(8,128)(2,1)} %collective-permute-done.11), channel_id=1, source_target_pairs={{0,30},{2,0},{4,2},{6,4},{8,6},{10,8},{12,10},{14,12},{16,14},{18,... | collective-permute-start | bytes 2162696 | tf_op jit(solution)/shard_map/ppermute | solution.py:90
  143.2 28.9 %collective-permute-start.6 = (bf16[128,2816]{1,0:T(8,128)(2,1)}, bf16[128,2816]{1,0:T(8,128)(2,1)}, u32[]{:S(2)}, u32[]{:S(2)}) collective-permute-start(bf16[128,2816]{1,0:T(8,128)(2,1)} %collective-permute-done.5), channel_id=1, source_target_pairs={{0,2},{2,4},{4,6},{6,8},{8,10},{10,12},{12,14},{14,16},{16,18},{18... | collective-permute-start | bytes 2162696 | tf_op jit(solution)/shard_map/ppermute | solution.py:88
  144.9 162.6 %copy-start.30 = (f32[2048]{0:T(1024)}, f32[2048]{0:T(1024)S(1)}, u32[]{:S(2)}) copy-start(f32[2048]{0:T(1024)S(1)} %slice_reduce_fusion) | copy-start | bytes 24580
  154.2 312.4 %copy-start = (bf16[128,2048]{1,0:T(8,128)(2,1)}, bf16[128,2048]{1,0:T(8,128)(2,1)S(1)}, u32[]{:S(2)}) copy-start(bf16[128,2048]{1,0:T(8,128)(2,1)S(1)} %all_gather.50) | copy-start | bytes 1572868
  167.5 82.9 %collective-permute-start.13 = (bf16[128,2816]{1,0:T(8,128)(2,1)}, bf16[128,2816]{1,0:T(8,128)(2,1)}, u32[]{:S(2)}, u32[]{:S(2)}) collective-permute-start(bf16[128,2816]{1,0:T(8,128)(2,1)} %collective-permute-done.12), channel_id=1, source_target_pairs={{0,30},{2,0},{4,2},{6,4},{8,6},{10,8},{12,10},{14,12},{16,14},{18,... | collective-permute-start | bytes 2162696 | tf_op jit(solution)/shard_map/ppermute | solution.py:90
  172.1 78.7 %collective-permute-start.7 = (bf16[128,2816]{1,0:T(8,128)(2,1)}, bf16[128,2816]{1,0:T(8,128)(2,1)}, u32[]{:S(2)}, u32[]{:S(2)}) collective-permute-start(bf16[128,2816]{1,0:T(8,128)(2,1)} %collective-permute-done.6), channel_id=1, source_target_pairs={{0,2},{2,4},{4,6},{6,8},{8,10},{10,12},{12,14},{14,16},{16,18},{18... | collective-permute-start | bytes 2162696 | tf_op jit(solution)/shard_map/ppermute | solution.py:88
  250.3 57.1 %copy-start.37 = (f32[128]{0:T(128)}, f32[128]{0:T(128)S(1)}, u32[]{:S(2)}) copy-start(f32[128]{0:T(128)S(1)} %add_rsqrt_fusion.2) | copy-start | bytes 1540
  250.4 57.1 %copy-start.45 = (f32[128]{0:T(128)}, f32[128]{0:T(128)S(1)}, u32[]{:S(2)}) copy-start(f32[128]{0:T(128)S(1)} %convert_subtract_fusion) | copy-start | bytes 1540
  250.4 57.1 %copy-start.34 = (f32[2048]{0:T(1024)}, f32[2048]{0:T(1024)S(1)}, u32[]{:S(2)}) copy-start(f32[2048]{0:T(1024)S(1)} %broadcast_subtract_fusion) | copy-start | bytes 24580
  250.4 27.6 %collective-permute-start.14 = (bf16[128,2816]{1,0:T(8,128)(2,1)}, bf16[128,2816]{1,0:T(8,128)(2,1)S(1)}, u32[]{:S(2)}, u32[]{:S(2)}) collective-permute-start(bf16[128,2816]{1,0:T(8,128)(2,1)} %collective-permute-done.13), channel_id=1, source_target_pairs={{0,30},{2,0},{4,2},{6,4},{8,6},{10,8},{12,10},{14,12},{16,14},{18,... | collective-permute-start | bytes 2162696 | tf_op jit(solution)/shard_map/ppermute | solution.py:90
  307.4 81.8 %copy-start.15 = (f32[128,2048]{1,0:T(8,128)}, f32[128,2048]{1,0:T(8,128)S(1)}, u32[]{:S(2)}) copy-start(f32[128,2048]{1,0:T(8,128)S(1)} %fusion.50) | copy-start | bytes 3145732
  314.2 117.8 %copy-start.9 = (f32[128,2048]{1,0:T(8,128)}, f32[128,2048]{1,0:T(8,128)S(1)}, u32[]{:S(2)}) copy-start(f32[128,2048]{1,0:T(8,128)S(1)} %get-tuple-element.282) | copy-start | bytes 3145732
  388.1 72.3 %copy-start.38 = (f32[128]{0:T(128)S(1)}, f32[128]{0:T(128)}, u32[]{:S(2)}) copy-start(f32[128]{0:T(128)} %copy-done.37) | copy-start | bytes 1540
  388.1 72.3 %copy-start.41 = (f32[16,1,128]{2,1,0:T(1,128)S(1)}, f32[16,1,128]{2,1,0:T(1,128)}, u32[]{:S(2)}) copy-start(f32[16,1,128]{2,1,0:T(1,128)} %convert_element_type.94) | copy-start | bytes 24580
  485.7 107.2 %slice-start = ((s8[11534336]{0:T(1024)(128)(4,1)}), s8[3145728]{0:T(1024)(128)(4,1)S(1)}, s32[]{:S(2)}) async-start(s8[11534336]{0:T(1024)(128)(4,1)} %bitcast.74), calls=%async_computation.25 | async-start | bytes 6291456
  596.8 54.6 %copy-start.7 = (f32[128,2048]{1,0:T(8,128)S(1)}, f32[128,2048]{1,0:T(8,128)}, u32[]{:S(2)}) copy-start(f32[128,2048]{1,0:T(8,128)} %copy-done.6) | copy-start | bytes 3145732
  606.2 461.6 %reduce-scatter.10.cloned.1.call-start = ((), (), s32[]{:S(2)}) async-start(), calls=%async_computation.15 | async-start | bytes 786432 | tf_op jit(solution)/shard_map/reduce_scatter | solution.py:152
  646.5 425.1 %reduce-scatter.20.cloned.1.call-start = ((), (), s32[]{:S(2)}) async-start(), calls=%async_computation.21 | async-start | bytes 208896 | tf_op jit(solution)/shard_map/reduce_scatter | solution.py:231
  737.5 159.9 %copy-start.31 = (f32[2048]{0:T(1024)S(1)}, f32[2048]{0:T(1024)}, u32[]{:S(2)}) copy-start(f32[2048]{0:T(1024)} %copy-done.30) | copy-start | bytes 24580
  737.5 159.9 %copy-start.35 = (f32[2048]{0:T(1024)S(1)}, f32[2048]{0:T(1024)}, u32[]{:S(2)}) copy-start(f32[2048]{0:T(1024)} %copy-done.34) | copy-start | bytes 24580
  754.0 147.7 %copy-start.33 = (f32[2048]{0:T(1024)S(1)}, f32[2048]{0:T(1024)}, u32[]{:S(2)}) copy-start(f32[2048]{0:T(1024)} %copy-done.32) | copy-start | bytes 24580
  760.4 144.6 %copy-start.1 = (bf16[128,2048]{1,0:T(8,128)(2,1)S(1)}, bf16[128,2048]{1,0:T(8,128)(2,1)}, u32[]{:S(2)}) copy-start(bf16[128,2048]{1,0:T(8,128)(2,1)} %copy-done) | copy-start | bytes 1572868
  905.0 233.4 %reduce-scatter.14.cloned.1.call-start = ((), (), s32[]{:S(2)}) async-start(), calls=%async_computation.18 | async-start | bytes 17825792 | tf_op jit(solution)/shard_map/reduce_scatter | solution.py:226
  914.0 406.6 %reduce-scatter.12.cloned.1.call-start = ((), (), s32[]{:S(2)}) async-start(), calls=%async_computation.17 | async-start | bytes 17825792 | tf_op jit(solution)/shard_map/reduce_scatter | solution.py:225
  923.5 579.3 %reduce-scatter.18.cloned.1.call-start = ((), (), s32[]{:S(2)}) async-start(), calls=%async_computation.20 | async-start | bytes 17825792 | tf_op jit(solution)/shard_map/reduce_scatter | solution.py:228
  932.8 752.3 %reduce-scatter.16.cloned.1.call-start = ((), (), s32[]{:S(2)}) async-start(), calls=%async_computation.19 | async-start | bytes 17825792 | tf_op jit(solution)/shard_map/reduce_scatter | solution.py:227
  942.1 973.4 %reduce-scatter.22.cloned.1.call-start = ((), (), s32[]{:S(2)}) async-start(), calls=%async_computation.22 | async-start | bytes 24510464 | tf_op jit(solution)/shard_map/reduce_scatter | solution.py:169
  953.0 1192.9 %reduce-scatter.24.cloned.1.call-start = ((), (), s32[]{:S(2)}) async-start(), calls=%async_computation.23 | async-start | bytes 24510464 | tf_op jit(solution)/shard_map/reduce_scatter | solution.py:170
  963.6 1412.8 %reduce-scatter.26.cloned.1.call-start = ((), (), s32[]{:S(2)}) async-start(), calls=%async_computation.24 | async-start | bytes 24510464 | tf_op jit(solution)/shard_map/reduce_scatter | solution.py:171
  978.4 91.1 %copy-start.12 = (f32[128,2048]{1,0:T(8,128)S(1)}, f32[128,2048]{1,0:T(8,128)}, u32[]{:S(2)}) copy-start(f32[128,2048]{1,0:T(8,128)} %copy-done.10) | copy-start | bytes 3145732
  (33 other events, 562.9 us)
Sparse Core Ops, SparseCore 0:
  10.2 114.5 all-gather.15
  127.0 94.1 all-gather.13
  223.4 83.7 all-gather.17
  309.2 73.1 all-gather.19
  384.5 94.1 all-gather.21
  480.7 95.6 all-gather.23
  606.3 38.2 all-reduce.63
  646.9 14.5 reduce-scatter.9
  905.1 51.2 reduce-scatter.19
  960.9 177.3 reduce-scatter.13
  1143.0 177.6 reduce-scatter.11
  1325.2 177.5 reduce-scatter.17
  1507.5 177.5 reduce-scatter.15
  1689.6 225.8 reduce-scatter.21
  1920.0 225.7 reduce-scatter.23
  2150.4 225.9 reduce-scatter.25
